TPU v7x, 32 devices: a whole 2x2x4 slice. The times are simulated.
32 devices in a mesh: dp: 8 (over y, x, core), mp: 4 (over z).
Axes of the slice: x: 2, y: 2, z: 4, core: 2. Of those that a mesh axis runs over, the one named last changes fastest.
Arguments:
- patches: bfloat16 [8192, 768], P('dp'), may hold values from -6 to 6
- attention_gain: bfloat16 [768], replicated, may hold values from 0.5 to 1.5
- query_weight: bfloat16 [768, 768], P(None, 'mp'), may hold values from -0.0390625 to 0.0390625
- key_weight: bfloat16 [768, 768], P(None, 'mp'), may hold values from -0.3125 to 0.3125
- value_weight: bfloat16 [768, 768], P(None, 'mp'), may hold values from -0.21875 to 0.21875
- output_weight: bfloat16 [768, 768], P('mp'), may hold values from -0.875 to 0.875
- feedforward_gain: bfloat16 [768], replicated, may hold values from 0.5 to 1.5
- gate_weight: bfloat16 [768, 2048], P(None, 'mp'), may hold values from -0.21875 to 0.21875
- up_weight: bfloat16 [768, 2048], P(None, 'mp'), may hold values from -0.21875 to 0.21875
- down_weight: bfloat16 [2048, 768], P('mp'), may hold values from -0.25 to 0.25
- cotangent: bfloat16 [8192, 768], P('dp'), may hold values from -6 to 6
- grid_extent: int32 [8, 2], P('dp'), may hold values from 16 to 32, as said below
Outputs:
- layer_output: bfloat16 [8192, 768], P('dp')
- input_grad: float32 [8192, 768], P('dp')
- attention_grad: float32 [768], P('dp')
- query_grad: float32 [768, 768], P('dp', 'mp')
- key_grad: float32 [768, 768], P('dp', 'mp')
- value_grad: float32 [768, 768], P('dp', 'mp')
- output_grad: float32 [768, 768], P('mp', 'dp')
- feedforward_grad: float32 [768], P('dp')
- gate_grad: float32 [768, 2048], P('dp', 'mp')
- up_grad: float32 [768, 2048], P('dp', 'mp')
- down_grad: float32 [2048, 768], P('mp', 'dp')
Inputs may be any that keep to these rules, and one draw needn't show every extreme that they name: `grid_extent`: chart 0 has all 32 rows and columns.
All inputs are finite; a program needn't handle non-finite values.
Results may differ from a plain program's by a relative error of at most 0.015.
Values may be sent and summed in bfloat16 or wider, within the bound.
A program may use at most 128 MiB of HBM per device.

v0:
```python
import jax
import jax.numpy as jnp
from jax import lax
from jax.sharding import PartitionSpec as P

HEAD = 64
epsilon = 1e-06
masked_score = -1000000000.0


def rms_scale(values, gain_vec):
    return (
        values * lax.rsqrt(jnp.mean(values * values, axis=-1, keepdims=True) + epsilon) * gain_vec
    )


def patch_valid(grid_extent, length):
    position = jnp.arange(length, dtype=jnp.int32)
    return position[None, :] < grid_extent[:, 0:1] * grid_extent[:, 1:2]


def query_blocks(length):
    block_rows = min(512, length)
    return (block_rows, jnp.arange(length // block_rows, dtype=jnp.int32) * block_rows)


def block_scores(query_block, keys_all, key_bias):
    scores = jnp.einsum("qhd,khd->hqk", query_block, keys_all, preferred_element_type=jnp.float32)
    return scores + key_bias


def attend_chart(chart_item):
    queries, keys_all, values_all, key_ok = chart_item
    block_rows, starts = query_blocks(queries.shape[0])
    key_bias = jnp.where(key_ok, 0.0, masked_score).astype(jnp.float32)

    def one_block(start):
        query_block = lax.dynamic_slice_in_dim(queries, start, block_rows, 0)
        scores = block_scores(query_block, keys_all, key_bias)
        highest = jnp.max(scores, axis=-1, keepdims=True)
        logsum = highest + jnp.log(jnp.sum(jnp.exp(scores - highest), axis=-1, keepdims=True))
        probs = jnp.exp(scores - logsum).astype(jnp.bfloat16)
        context = jnp.einsum("hqk,khd->qhd", probs, values_all, preferred_element_type=jnp.float32)
        return (context.astype(jnp.bfloat16), logsum)

    context, logsum = lax.map(one_block, starts)
    return (context.reshape(queries.shape), logsum)


def attend_back(chart_item):
    queries, keys_all, values_all, key_ok, logsum, context_back = chart_item
    block_rows, starts = query_blocks(queries.shape[0])
    key_bias = jnp.where(key_ok, 0.0, masked_score).astype(jnp.float32)

    def one_block(carry, block_item):
        key_total, value_total = carry
        start, block_logsum = block_item
        query_block = lax.dynamic_slice_in_dim(queries, start, block_rows, 0)
        grad_block = lax.dynamic_slice_in_dim(context_back, start, block_rows, 0)
        probs_full = jnp.exp(block_scores(query_block, keys_all, key_bias) - block_logsum)
        value_total = value_total + jnp.einsum(
            "hqk,qhd->khd",
            probs_full.astype(jnp.bfloat16),
            grad_block,
            preferred_element_type=jnp.float32,
        )
        probs_back = jnp.einsum(
            "qhd,khd->hqk", grad_block, values_all, preferred_element_type=jnp.float32
        )
        score_back = probs_full * (
            probs_back - jnp.sum(probs_full * probs_back, axis=-1, keepdims=True)
        )
        score_back = score_back.astype(jnp.bfloat16)
        query_part = jnp.einsum(
            "hqk,khd->qhd", score_back, keys_all, preferred_element_type=jnp.float32
        )
        key_total = key_total + jnp.einsum(
            "hqk,qhd->khd", score_back, query_block, preferred_element_type=jnp.float32
        )
        return ((key_total, value_total), query_part.astype(jnp.bfloat16))

    zeros_keys = jnp.zeros(keys_all.shape, jnp.float32)
    (key_total, value_total), query_back = lax.scan(
        one_block, (zeros_keys, zeros_keys), (starts, logsum)
    )
    return (
        query_back.reshape(queries.shape),
        key_total.astype(jnp.bfloat16),
        value_total.astype(jnp.bfloat16),
    )


def layer_forward(inputs, weights, valid_mask, attention_total):
    (
        first_gain,
        query_weight,
        key_weight,
        value_weight,
        output_weight,
        second_gain,
        gate_weight,
        up_weight,
        down_weight,
    ) = weights
    rows_total = inputs.shape[0]
    charts = valid_mask.shape[0]
    length = rows_total // charts
    normed_one = rms_scale(inputs, first_gain).astype(jnp.bfloat16)

    def project(matrix):
        product = jnp.dot(normed_one, matrix, preferred_element_type=jnp.float32)
        return product.astype(jnp.bfloat16).reshape(charts, length, matrix.shape[1] // HEAD, HEAD)

    queries = project(query_weight)
    keys_all = project(key_weight)
    values_all = project(value_weight)
    context, logsum = lax.map(attend_chart, (queries, keys_all, values_all, valid_mask))
    context = context.reshape(rows_total, query_weight.shape[1])
    attention_out = attention_total(
        jnp.dot(context, output_weight, preferred_element_type=jnp.float32)
    )
    hidden = inputs + attention_out
    normed_two = rms_scale(hidden, second_gain).astype(jnp.bfloat16)
    gate_pre = jnp.dot(normed_two, gate_weight, preferred_element_type=jnp.float32)
    up_pre = jnp.dot(normed_two, up_weight, preferred_element_type=jnp.float32)
    mixed = (jax.nn.gelu(gate_pre, approximate=True) * up_pre).astype(jnp.bfloat16)
    return (
        normed_one,
        queries,
        keys_all,
        values_all,
        logsum,
        context,
        hidden,
        normed_two,
        gate_pre,
        up_pre,
        mixed,
    )


def gelu_product(gate_pre, up_pre):
    return jax.nn.gelu(gate_pre, approximate=True) * up_pre


def body(
    patches,
    attention_gain,
    query_weight,
    key_weight,
    value_weight,
    output_weight,
    feedforward_gain,
    gate_weight,
    up_weight,
    down_weight,
    cotangent,
    grid_extent,
):
    rows_total = patches.shape[0]
    charts = grid_extent.shape[0]
    length = rows_total // charts
    valid_mask = patch_valid(grid_extent, length)
    row_keep = valid_mask.reshape(rows_total, 1)
    inputs = patches.astype(jnp.float32)
    first_gain = attention_gain.astype(jnp.float32)
    second_gain = feedforward_gain.astype(jnp.float32)
    weights = (
        first_gain,
        query_weight,
        key_weight,
        value_weight,
        output_weight,
        second_gain,
        gate_weight,
        up_weight,
        down_weight,
    )

    def attention_total(partial_value):
        share = lax.psum_scatter(partial_value, "mp", scatter_dimension=0, tiled=True)
        return lax.all_gather(share, "mp", axis=0, tiled=True)

    def attention_repeat(partial_value):
        share = lax.psum_scatter(partial_value, "mp", scatter_dimension=0, tiled=True)
        return lax.all_gather(share, "mp", axis=0, tiled=True)

    first_pass = layer_forward(inputs, weights, valid_mask, attention_total)
    feedforward_share = lax.psum_scatter(
        jnp.dot(first_pass[10], down_weight, preferred_element_type=jnp.float32),
        "mp",
        scatter_dimension=0,
        tiled=True,
    )
    rows_here = feedforward_share.shape[0]
    row_start = lax.axis_index("mp") * rows_here
    hidden_here = lax.dynamic_slice_in_dim(first_pass[6], row_start, rows_here, 0)
    keep_here = lax.dynamic_slice_in_dim(row_keep, row_start, rows_here, 0)
    output_here = jnp.where(keep_here, hidden_here + feedforward_share, 0.0).astype(jnp.bfloat16)
    layer_output = lax.all_gather(output_here, "mp", axis=0, tiled=True)
    saved = layer_forward(inputs, weights, valid_mask, attention_repeat)
    (
        normed_one,
        queries,
        keys_all,
        values_all,
        logsum,
        context,
        hidden,
        normed_two,
        gate_pre,
        up_pre,
        mixed,
    ) = saved
    out_back = jnp.where(row_keep, cotangent.astype(jnp.float32), 0.0)
    out_low = out_back.astype(jnp.bfloat16)
    down_grad = jnp.einsum("rf,rd->fd", mixed, out_low, preferred_element_type=jnp.float32)
    mixed_back = jnp.einsum("rd,fd->rf", out_low, down_weight, preferred_element_type=jnp.float32)
    _, gelu_pull = jax.vjp(gelu_product, gate_pre, up_pre)
    gate_back, up_back = gelu_pull(mixed_back)
    gate_back = gate_back.astype(jnp.bfloat16)
    up_back = up_back.astype(jnp.bfloat16)
    gate_grad = jnp.einsum("rd,rf->df", normed_two, gate_back, preferred_element_type=jnp.float32)
    up_grad = jnp.einsum("rd,rf->df", normed_two, up_back, preferred_element_type=jnp.float32)
    normed_two_part = jnp.einsum(
        "rf,df->rd", gate_back, gate_weight, preferred_element_type=jnp.float32
    ) + jnp.einsum("rf,df->rd", up_back, up_weight, preferred_element_type=jnp.float32)
    normed_two_share = lax.psum_scatter(normed_two_part, "mp", scatter_dimension=0, tiled=True)
    normed_two_back = lax.all_gather(normed_two_share, "mp", axis=0, tiled=True)
    _, second_pull = jax.vjp(rms_scale, hidden, second_gain)
    hidden_part, second_gain_grad = second_pull(normed_two_back)
    hidden_back = out_back + hidden_part
    second_gain_grad, gate_grad, up_grad = (
        lax.psum_scatter(second_gain_grad, "dp", scatter_dimension=0, tiled=True),
        lax.psum_scatter(gate_grad, "dp", scatter_dimension=0, tiled=True),
        lax.psum_scatter(up_grad, "dp", scatter_dimension=0, tiled=True),
    )
    down_grad = lax.psum_scatter(down_grad, "dp", scatter_dimension=1, tiled=True)
    hidden_low = hidden_back.astype(jnp.bfloat16)
    output_grad = jnp.einsum("rc,rd->cd", context, hidden_low, preferred_element_type=jnp.float32)
    context_back = jnp.einsum(
        "rd,cd->rc", hidden_low, output_weight, preferred_element_type=jnp.float32
    )
    context_back = context_back.astype(jnp.bfloat16).reshape(queries.shape)
    query_back, key_back, value_back = lax.map(
        attend_back, (queries, keys_all, values_all, valid_mask, logsum, context_back)
    )
    features_here = query_weight.shape[1]
    query_back = query_back.reshape(rows_total, features_here)
    key_back = key_back.reshape(rows_total, features_here)
    value_back = value_back.reshape(rows_total, features_here)
    query_grad = jnp.einsum("rd,rc->dc", normed_one, query_back, preferred_element_type=jnp.float32)
    key_grad = jnp.einsum("rd,rc->dc", normed_one, key_back, preferred_element_type=jnp.float32)
    value_grad = jnp.einsum("rd,rc->dc", normed_one, value_back, preferred_element_type=jnp.float32)
    normed_one_part = (
        jnp.einsum("rc,dc->rd", query_back, query_weight, preferred_element_type=jnp.float32)
        + jnp.einsum("rc,dc->rd", key_back, key_weight, preferred_element_type=jnp.float32)
        + jnp.einsum("rc,dc->rd", value_back, value_weight, preferred_element_type=jnp.float32)
    )
    normed_one_share = lax.psum_scatter(normed_one_part, "mp", scatter_dimension=0, tiled=True)
    normed_one_back = lax.all_gather(normed_one_share, "mp", axis=0, tiled=True)
    _, first_pull = jax.vjp(rms_scale, inputs, first_gain)
    input_part, first_gain_grad = first_pull(normed_one_back)
    input_grad = hidden_back + input_part
    first_gain_grad, query_grad, key_grad, value_grad = (
        lax.psum_scatter(first_gain_grad, "dp", scatter_dimension=0, tiled=True),
        lax.psum_scatter(query_grad, "dp", scatter_dimension=0, tiled=True),
        lax.psum_scatter(key_grad, "dp", scatter_dimension=0, tiled=True),
        lax.psum_scatter(value_grad, "dp", scatter_dimension=0, tiled=True),
    )
    output_grad = lax.psum_scatter(output_grad, "dp", scatter_dimension=1, tiled=True)
    return (
        layer_output,
        input_grad,
        first_gain_grad,
        query_grad,
        key_grad,
        value_grad,
        output_grad,
        second_gain_grad,
        gate_grad,
        up_grad,
        down_grad,
    )


def solution(mesh):
    placed = (
        P("dp", None),
        P(),
        P(None, "mp"),
        P(None, "mp"),
        P(None, "mp"),
        P("mp", None),
        P(),
        P(None, "mp"),
        P(None, "mp"),
        P("mp", None),
        P("dp", None),
        P("dp", None),
    )
    return jax.shard_map(
        body,
        mesh=mesh,
        in_specs=placed,
        out_specs=(
            P("dp", None),
            P("dp", None),
            P("dp"),
            P("dp", "mp"),
            P("dp", "mp"),
            P("dp", "mp"),
            P("mp", "dp"),
            P("dp"),
            P("dp", "mp"),
            P("dp", "mp"),
            P("mp", "dp"),
        ),
        check_vma=False,
    )
```

profile of v0, /device:TPU:0, one launch (start us, length us, event | category | flops | bytes accessed | tf_op | source)
XLA Modules:
  0.0 994.6 jit_solution(6283610246792495754)
XLA Ops:
  16.5 12.8 %while.67 = (s32[]{:T(128)}, bf16[2,512,3,64]{1,3,2,0:T(8,128)(2,1)S(1)}, f32[2,3,512,1]{2,1,3,0:T(4,128)S(1)}, s32[2]{0:T(128)S(1)}, bf16[1024,3,64]{0,2,1:T(8,...) while((s32[]{:T(128)}, ...), condition=%wide.region_11.12_spmd.clone, body=%wide.region_8.11_spmd.clone.sunk | while | flops 415334912 | bytes 20129972 | solution.py:46
  33.3 63.0 %reduce-scatter.19.cloned.1.call-done = f32[256,768]{1,0:T(8,128)} async-done(((f32[1024,768]{1,0:T(8,128)}), f32[256,768]{1,0:T(8,128)}) %reduce-scatter.19.cloned.1.call-update) | async-done | bytes 786448 | tf_op jit(solution)/shard_map/reduce_scatter | solution.py:185
  96.5 65.0 %all-gather.10.cloned.1.call-done = f32[1024,768]{1,0:T(8,128)} async-done(((f32[256,768]{1,0:T(8,128)}), f32[1024,768]{1,0:T(8,128)}) %all-gather.10.cloned.1.call-update) | async-done | bytes 3145744 | tf_op jit(solution)/shard_map/all_gather | solution.py:186
  175.9 59.0 %reduce-scatter.21.cloned.1.call-done = f32[256,768]{1,0:T(8,128)} async-done(((f32[1024,768]{1,0:T(8,128)}), f32[256,768]{1,0:T(8,128)}) %reduce-scatter.21.cloned.1.call-update) | async-done | bytes 786448 | tf_op jit(solution)/shard_map/reduce_scatter | solution.py:228
  235.5 64.4 %all-gather.12.cloned.1.call-done = f32[1024,768]{1,0:T(8,128)} async-done(((f32[256,768]{1,0:T(8,128)}), f32[1024,768]{1,0:T(8,128)}) %all-gather.12.cloned.1.call-update) | async-done | bytes 3145744 | tf_op jit(solution)/shard_map/all_gather | solution.py:229
  310.5 24.8 %while.68 = (s32[]{:T(128)}, f32[1024,3,64]{0,2,1:T(8,128)S(1)}, f32[1024,3,64]{0,2,1:T(8,128)}, bf16[2,512,3,64]{1,3,2,0:T(8,128)(2,1)}, s32[2]{0:T(128)}, /*in...) while((s32[]{:T(128)}, f32[1024,3,64]{0,2,1:T(8,128)S(1)}, ...), condition=%wide.region_18.19_spmd.clone, body=%wide.region_16.18_spmd.clone.sunk | while | flops 1026392576 | bytes 66714016 | solution.py:83
  342.1 14.3 %while.66 = (s32[]{:T(128)}, bf16[2,512,3,64]{1,3,2,0:T(8,128)(2,1)}, s32[2]{0:T(128)S(1)}, bf16[1024,3,64]{0,2,1:T(8,128)(2,1)S(1)}, bf16[1024,3,64]{0,2,1:T(8,...) while((s32[]{:T(128)}, ...), condition=%wide.region_4.5_spmd.clone, body=%wide.region_1.4_spmd.clone.sunk | while | flops 415334912 | bytes 23261408 | solution.py:46
  361.2 38.9 %reduce-scatter.23.cloned.1.call-done = f32[256,768]{1,0:T(8,128)} async-done(((f32[1024,768]{1,0:T(8,128)}), f32[256,768]{1,0:T(8,128)}) %reduce-scatter.23.cloned.1.call-update) | async-done | bytes 786448 | tf_op jit(solution)/shard_map/reduce_scatter | solution.py:260
  400.2 63.0 %reduce-scatter.15.cloned.1.call-done = f32[256,768]{1,0:T(8,128)} async-done(((f32[1024,768]{1,0:T(8,128)}), f32[256,768]{1,0:T(8,128)}) %reduce-scatter.15.cloned.1.call-update) | async-done | bytes 786448 | tf_op jit(solution)/shard_map/reduce_scatter | solution.py:181
  463.2 65.1 %all-gather.14.cloned.1.call-done = f32[1024,768]{1,0:T(8,128)} async-done(((f32[256,768]{1,0:T(8,128)}), f32[1024,768]{1,0:T(8,128)}) %all-gather.14.cloned.1.call-update) | async-done | bytes 3145744 | tf_op jit(solution)/shard_map/all_gather | solution.py:261
  531.3 60.7 %all-gather.6.cloned.1.call-done = f32[1024,768]{1,0:T(8,128)} async-done(((f32[256,768]{1,0:T(8,128)}), f32[1024,768]{1,0:T(8,128)}) %all-gather.6.cloned.1.call-update) | async-done | bytes 3145744 | tf_op jit(solution)/shard_map/all_gather | solution.py:182
  592.0 5.6 multiply_reduce_fusion.4
  601.7 6.3 fusion.72
  612.6 54.5 %reduce-scatter.17.cloned.1.call-done = f32[256,768]{1,0:T(8,128)} async-done(((f32[1024,768]{1,0:T(8,128)}), f32[256,768]{1,0:T(8,128)}) %reduce-scatter.17.cloned.1.call-update) | async-done | bytes 786448 | tf_op jit(solution)/shard_map/reduce_scatter | solution.py:189
  669.6 5.5 fusion.73
  688.8 16.3 %reduce-scatter.37.cloned.1.call-done = f32[96,192]{1,0:T(8,128)} async-done(((f32[768,192]{1,0:T(8,128)}), f32[96,192]{1,0:T(8,128)}) %reduce-scatter.37.cloned.1.call-update) | async-done | bytes 73744
  706.7 12.6 %all-reduce.2 = (f32[768]{0:T(1024)S(1)}, f32[768]{0:T(1024)S(1)}) all-reduce(f32[768]{0:T(1024)S(1)} %get-tuple-element.302, f32[768]{0:T(1024)S(1)} %copy-done.60), channel_id=7, replica_groups=mesh['dp'=8,'mp'=4] {'dp'}, use_global_device_ids=true, to_apply=%region_22.23.clone | all-reduce | flops 1536 | bytes 12288
  720.5 23.3 %all-gather.8.cloned.1.call-done = bf16[1024,768]{1,0:T(8,128)(2,1)} async-done(((bf16[256,768]{1,0:T(8,128)(2,1)}), bf16[1024,768]{1,0:T(8,128)(2,1)}) %all-gather.8.cloned.1.call-update) | async-done | bytes 1572880 | tf_op jit(solution)/shard_map/all_gather | solution.py:200
  743.8 41.1 %reduce-scatter.35.cloned.1.call-done = f32[512,96]{0,1:T(8,128)} async-done(((f32[512,768]{0,1:T(8,128)}), f32[512,96]{0,1:T(8,128)}) %reduce-scatter.35.cloned.1.call-update) | async-done | bytes 196624 | tf_op jit(solution)/shard_map/reduce_scatter | solution.py:238
  784.9 42.4 %reduce-scatter.31.cloned.1.call-done = f32[96,512]{1,0:T(8,128)} async-done(((f32[768,512]{1,0:T(8,128)}), f32[96,512]{1,0:T(8,128)}) %reduce-scatter.31.cloned.1.call-update) | async-done | bytes 196624 | tf_op jit(solution)/shard_map/reduce_scatter | solution.py:235
  827.2 42.2 %reduce-scatter.33.cloned.1.call-done = f32[96,512]{1,0:T(8,128)} async-done(((f32[768,512]{1,0:T(8,128)}), f32[96,512]{1,0:T(8,128)}) %reduce-scatter.33.cloned.1.call-update) | async-done | bytes 196624 | tf_op jit(solution)/shard_map/reduce_scatter | solution.py:236
  869.5 38.6 %reduce-scatter.29.cloned.1.call-done = f32[96,192]{1,0:T(8,128)} async-done(((f32[768,192]{1,0:T(8,128)}), f32[96,192]{1,0:T(8,128)}) %reduce-scatter.29.cloned.1.call-update) | async-done | bytes 73744 | tf_op jit(solution)/shard_map/reduce_scatter | solution.py:269
  908.0 38.6 %reduce-scatter.25.cloned.1.call-done = f32[96,192]{1,0:T(8,128)} async-done(((f32[768,192]{1,0:T(8,128)}), f32[96,192]{1,0:T(8,128)}) %reduce-scatter.25.cloned.1.call-update) | async-done | bytes 73744 | tf_op jit(solution)/shard_map/reduce_scatter | solution.py:267
  946.6 38.6 %reduce-scatter.27.cloned.1.call-done = f32[96,192]{1,0:T(8,128)} async-done(((f32[768,192]{1,0:T(8,128)}), f32[96,192]{1,0:T(8,128)}) %reduce-scatter.27.cloned.1.call-update) | async-done | bytes 73744 | tf_op jit(solution)/shard_map/reduce_scatter | solution.py:268
  (297 shorter events, 120.9 us)
Async XLA Ops:
  7.2 159.5 %copy-start = (bf16[768,512]{1,0:T(8,128)(2,1)S(1)}, bf16[768,512]{1,0:T(8,128)(2,1)}, u32[]{:S(2)}) copy-start(bf16[768,512]{1,0:T(8,128)(2,1)} %param.26) | copy-start | bytes 2359300
  7.2 89.2 %reduce-scatter.19.cloned.1.call-start = ((), (), s32[]{:S(2)}) async-start(), calls=%async_computation.16 | async-start | bytes 3932160 | tf_op jit(solution)/shard_map/reduce_scatter | solution.py:185
  31.0 130.6 %copy-start.1 = (bf16[1024,768]{1,0:T(8,128)(2,1)S(1)}, bf16[1024,768]{1,0:T(8,128)(2,1)}, u32[]{:S(2)}) copy-start(bf16[1024,768]{1,0:T(8,128)(2,1)} %param.18) | copy-start | bytes 4718596
  33.3 128.2 %all-gather.10.cloned.1.call-start = ((), (), s32[]{:S(2)}) async-start(), calls=%async_computation.17 | async-start | bytes 3932160 | tf_op jit(solution)/shard_map/all_gather | solution.py:186
  96.4 138.5 %reduce-scatter.21.cloned.1.call-start = ((), (), s32[]{:S(2)}) async-start(), calls=%async_computation.18 | async-start | bytes 3932160 | tf_op jit(solution)/shard_map/reduce_scatter | solution.py:228
  96.5 68.4 %copy-start.47 = (f32[768]{0:T(1024)}, f32[768]{0:T(1024)S(1)}, u32[]{:S(2)}) copy-start(f32[768]{0:T(1024)S(1)} %convert_element_type.102) | copy-start | bytes 9220
  96.5 71.2 %copy-start.62 = (pred[1024]{0:T(1024)(128)(4,1)}, pred[1024]{0:T(1024)(128)(4,1)S(1)}, u32[]{:S(2)}) copy-start(pred[1024]{0:T(1024)(128)(4,1)S(1)} %iota_compare_fusion.3) | copy-start | bytes 3076
  175.9 124.0 %all-gather.12.cloned.1.call-start = ((), (), s32[]{:S(2)}) async-start(), calls=%async_computation.19 | async-start | bytes 3932160 | tf_op jit(solution)/shard_map/all_gather | solution.py:229
  235.0 165.2 %reduce-scatter.23.cloned.1.call-start = ((), (), s32[]{:S(2)}) async-start(), calls=%async_computation.20 | async-start | bytes 3932160 | tf_op jit(solution)/shard_map/reduce_scatter | solution.py:260
  341.1 122.1 %reduce-scatter.15.cloned.1.call-start = ((), (), s32[]{:S(2)}) async-start(), calls=%async_computation.12 | async-start | bytes 3932160 | tf_op jit(solution)/shard_map/reduce_scatter | solution.py:181
  361.1 167.2 %copy-start.51 = (f32[768]{0:T(1024)S(1)}, f32[768]{0:T(1024)}, u32[]{:S(2)}) copy-start(f32[768]{0:T(1024)} %copy-done.50) | copy-start | bytes 9220
  361.1 167.2 %copy-start.53 = (f32[1024]{0:T(1024)S(1)}, f32[1024]{0:T(1024)}, u32[]{:S(2)}) copy-start(f32[1024]{0:T(1024)} %copy-done.52) | copy-start | bytes 12292
  361.2 167.1 %all-gather.14.cloned.1.call-start = ((), (), s32[]{:S(2)}) async-start(), calls=%async_computation.21 | async-start | bytes 3932160 | tf_op jit(solution)/shard_map/all_gather | solution.py:261
  400.1 131.2 %copy-start.57 = (f32[1024]{0:T(1024)S(1)}, f32[1024]{0:T(1024)}, u32[]{:S(2)}) copy-start(f32[1024]{0:T(1024)} %copy-done.56) | copy-start | bytes 12292
  400.1 191.9 %all-gather.6.cloned.1.call-start = ((), (), s32[]{:S(2)}) async-start(), calls=%async_computation.13 | async-start | bytes 3932160 | tf_op jit(solution)/shard_map/all_gather | solution.py:182
  463.2 203.9 %reduce-scatter.17.cloned.1.call-start = ((), (), s32[]{:S(2)}) async-start(), calls=%async_computation.14 | async-start | bytes 3932160 | tf_op jit(solution)/shard_map/reduce_scatter | solution.py:189
  608.0 97.1 %reduce-scatter.37.cloned.1.call-start = ((), (), s32[]{:S(2)}) async-start(), calls=%async_computation.28 | async-start | bytes 884736
  612.5 131.3 %all-gather.8.cloned.1.call-start = ((), (), s32[]{:S(2)}) async-start(), calls=%async_computation.15 | async-start | bytes 1966080 | tf_op jit(solution)/shard_map/all_gather | solution.py:200
  669.3 115.6 %reduce-scatter.35.cloned.1.call-start = ((), (), s32[]{:S(2)}) async-start(), calls=%async_computation.27 | async-start | bytes 1769472 | tf_op jit(solution)/shard_map/reduce_scatter | solution.py:238
  675.1 152.1 %reduce-scatter.31.cloned.1.call-start = ((), (), s32[]{:S(2)}) async-start(), calls=%async_computation.25 | async-start | bytes 1769472 | tf_op jit(solution)/shard_map/reduce_scatter | solution.py:235
  678.6 190.8 %reduce-scatter.33.cloned.1.call-start = ((), (), s32[]{:S(2)}) async-start(), calls=%async_computation.26 | async-start | bytes 1769472 | tf_op jit(solution)/shard_map/reduce_scatter | solution.py:236
  682.8 225.3 %reduce-scatter.29.cloned.1.call-start = ((), (), s32[]{:S(2)}) async-start(), calls=%async_computation.24 | async-start | bytes 884736 | tf_op jit(solution)/shard_map/reduce_scatter | solution.py:269
  684.4 262.2 %reduce-scatter.25.cloned.1.call-start = ((), (), s32[]{:S(2)}) async-start(), calls=%async_computation.22 | async-start | bytes 884736 | tf_op jit(solution)/shard_map/reduce_scatter | solution.py:267
  686.0 299.3 %reduce-scatter.27.cloned.1.call-start = ((), (), s32[]{:S(2)}) async-start(), calls=%async_computation.23 | async-start | bytes 884736 | tf_op jit(solution)/shard_map/reduce_scatter | solution.py:268
  (74 other events, 453.2 us)
Sparse Core Ops, SparseCore 0:
  33.4 62.9 reduce-scatter.18
  98.0 63.5 all-gather.9
  176.0 58.8 reduce-scatter.20
  236.4 63.5 all-gather.11
  341.2 58.8 reduce-scatter.22
  402.8 60.2 reduce-scatter.14
  464.7 63.5 all-gather.13
  529.9 62.1 all-gather.5
  608.1 58.8 reduce-scatter.16
  670.0 35.0 reduce-scatter.36
  706.7 37.0 all-gather.7
  747.5 37.3 reduce-scatter.34
  788.7 38.4 reduce-scatter.30
  831.0 38.4 reduce-scatter.32
  873.0 34.9 reduce-scatter.28
  911.6 34.9 reduce-scatter.24
  950.2 34.9 reduce-scatter.26
where the time goes:
time: 1000 us; the launch traced here: 995 us
  waiting for transfers between devices  815 us (82%)
  matrix products  75.7 us (8%)
  other arithmetic  32.9 us (3%)
  local copies, waits for them, and re-layouts  28 us (3%)
  between operations  16.9 us (2%)
  blocking collectives  12.6 us (1%)
  loops' own time  12.1 us (1%)
    all_gather x1, waiting for transfers between devices, body(): normed_one_back = lax.all_gather(normed_one_share, 'mp', axis=0, tiled=True)  65.1 us
    all_gather x1, waiting for transfers between devices, attention_repeat(): return lax.all_gather(share, 'mp', axis=0, tiled=True)  65 us
    all_gather x1, waiting for transfers between devices, body(): normed_two_back = lax.all_gather(normed_two_share, 'mp', axis=0, tiled=True)  64.4 us
    reduce_scatter x1, waiting for transfers between devices, attention_repeat(): lax.psum_scatter(partial_value, 'mp', scatter_dimension=0, tiled=True)  63 us
    reduce_scatter x1, waiting for transfers between devices, attention_total(): lax.psum_scatter(partial_value, 'mp', scatter_dimension=0, tiled=True)  63 us
    all_gather x1, waiting for transfers between devices, attention_total(): return lax.all_gather(share, 'mp', axis=0, tiled=True)  60.7 us
    reduce_scatter x1, waiting for transfers between devices, body(): lax.psum_scatter(normed_two_part, 'mp', scatter_dimension=0, tiled=True)  59 us
    reduce_scatter x1, waiting for transfers between devices, body(): lax.psum_scatter(jnp.dot(first_pass[10], down_weight, preferred_element_t...  54.5 us
  transfers between devices with their start and end apart: 17, of which 17 were waited for; matrix products, arithmetic and copies ran while one was open for 4% of the time, Pallas kernels for 0%

commit v1 on v0

--- a/solution.py
+++ b/solution.py
@@ -197,7 +197,16 @@
     hidden_here = lax.dynamic_slice_in_dim(first_pass[6], row_start, rows_here, 0)
     keep_here = lax.dynamic_slice_in_dim(row_keep, row_start, rows_here, 0)
     output_here = jnp.where(keep_here, hidden_here + feedforward_share, 0.0).astype(jnp.bfloat16)
-    layer_output = lax.all_gather(output_here, "mp", axis=0, tiled=True)
+    ways = lax.axis_size("mp")
+    up = [(d, (d + 1) % ways) for d in range(ways)]
+    down = [(d, (d - 1) % ways) for d in range(ways)]
+    earlier, later = ([output_here], [output_here])
+    for __2 in range(ways // 2):
+        earlier.append(lax.ppermute(earlier[-1], "mp", up))
+    for __2 in range((ways - 1) // 2):
+        later.append(lax.ppermute(later[-1], "mp", down))
+    line = jnp.concatenate([*earlier[::-1], *later[1:]], axis=0)
+    layer_output = jnp.roll(line, (lax.axis_index("mp") - ways // 2) * output_here.shape[0], axis=0)
     saved = layer_forward(inputs, weights, valid_mask, attention_repeat)
     (
         normed_one,

time: 1000 us -> 964 us (0.964)
  waiting for transfers between devices: 815 us -> 769 us
    all_gather x1 -> x0, waiting for transfers between devices: 23.3 us -> none  [body(): layer_output = lax.all_gather(output_here, 'mp', axis=0, tiled=True)]
    reduce_scatter x1, waiting for transfers between devices: 41.1 us -> 21.4 us  [body(): lax.psum_scatter(down_grad, 'dp', scatter_dimension=1, tiled=True)]
    reduce_scatter x1, waiting for transfers between devices: 54.5 us -> 38.9 us  [body(): lax.psum_scatter(jnp.dot(first_pass[10], down_weight, preferred_element_t...]
    ppermute x0 -> x3, waiting for transfers between devices: none -> 11.5 us  [the longest x2 11.5 us: body(): earlier.append(lax.ppermute(earlier[-1], 'mp', up))]
  transfers between devices with their start and end apart: 17 -> 19, of which waited for: 17 -> 17; matrix products, arithmetic and copies ran while one was open for 4% -> 5% of each run, Pallas kernels for 0% -> 0%
where the time goes in v1:
time: 964 us; the launch traced here: 955 us
  waiting for transfers between devices  769 us (80%)
  matrix products  74.5 us (8%)
  other arithmetic  32.1 us (3%)
  local copies, waits for them, and re-layouts  31.1 us (3%)
  between operations  16.9 us (2%)
  blocking collectives  12.6 us (1%)
  loops' own time  12.1 us (1%)
    all_gather x1, waiting for transfers between devices, body(): normed_one_back = lax.all_gather(normed_one_share, 'mp', axis=0, tiled=True)  65 us
    all_gather x1, waiting for transfers between devices, attention_repeat(): return lax.all_gather(share, 'mp', axis=0, tiled=True)  65 us
    all_gather x1, waiting for transfers between devices, body(): normed_two_back = lax.all_gather(normed_two_share, 'mp', axis=0, tiled=True)  64.4 us
    reduce_scatter x1, waiting for transfers between devices, attention_repeat(): lax.psum_scatter(partial_value, 'mp', scatter_dimension=0, tiled=True)  63 us
    reduce_scatter x1, waiting for transfers between devices, attention_total(): lax.psum_scatter(partial_value, 'mp', scatter_dimension=0, tiled=True)  63 us
    all_gather x1, waiting for transfers between devices, attention_total(): return lax.all_gather(share, 'mp', axis=0, tiled=True)  60.7 us
    reduce_scatter x1, waiting for transfers between devices, body(): lax.psum_scatter(normed_two_part, 'mp', scatter_dimension=0, tiled=True)  59 us
    reduce_scatter x1, waiting for transfers between devices, body(): lax.psum_scatter(up_grad, 'dp', scatter_dimension=0, tiled=True)  42.4 us
  transfers between devices with their start and end apart: 19, of which 17 were waited for; matrix products, arithmetic and copies ran while one was open for 5% of the time, Pallas kernels for 0%

profile of v1, /device:TPU:0, one launch (start us, length us, event | category | flops | bytes accessed | tf_op | source)
XLA Modules:
  0.0 954.8 jit_solution(10973841947188669912)
XLA Ops:
  16.5 12.8 %while.67 = (s32[]{:T(128)}, bf16[2,512,3,64]{1,3,2,0:T(8,128)(2,1)S(1)}, f32[2,3,512,1]{2,1,3,0:T(4,128)S(1)}, s32[2]{0:T(128)S(1)}, bf16[1024,3,64]{0,2,1:T(8,...) while((s32[]{:T(128)}, ...), condition=%wide.region_11.12_spmd.clone, body=%wide.region_8.11_spmd.clone.sunk | while | flops 415334912 | bytes 20129972 | solution.py:46
  33.5 63.0 %reduce-scatter.19.cloned.1.call-done = f32[256,768]{1,0:T(8,128)} async-done(((f32[1024,768]{1,0:T(8,128)}), f32[256,768]{1,0:T(8,128)}) %reduce-scatter.19.cloned.1.call-update) | async-done | bytes 786448 | tf_op jit(solution)/shard_map/reduce_scatter | solution.py:185
  96.7 65.0 %all-gather.7.cloned.1.call-done = f32[1024,768]{1,0:T(8,128)} async-done(((f32[256,768]{1,0:T(8,128)}), f32[1024,768]{1,0:T(8,128)}) %all-gather.7.cloned.1.call-update) | async-done | bytes 3145744 | tf_op jit(solution)/shard_map/all_gather | solution.py:186
  176.2 59.0 %reduce-scatter.21.cloned.1.call-done = f32[256,768]{1,0:T(8,128)} async-done(((f32[1024,768]{1,0:T(8,128)}), f32[256,768]{1,0:T(8,128)}) %reduce-scatter.21.cloned.1.call-update) | async-done | bytes 786448 | tf_op jit(solution)/shard_map/reduce_scatter | solution.py:237
  235.8 64.4 %all-gather.9.cloned.1.call-done = f32[1024,768]{1,0:T(8,128)} async-done(((f32[256,768]{1,0:T(8,128)}), f32[1024,768]{1,0:T(8,128)}) %all-gather.9.cloned.1.call-update) | async-done | bytes 3145744 | tf_op jit(solution)/shard_map/all_gather | solution.py:238
  310.8 24.9 %while.68 = (s32[]{:T(128)}, f32[1024,3,64]{0,2,1:T(8,128)S(1)}, f32[1024,3,64]{0,2,1:T(8,128)}, bf16[2,512,3,64]{1,3,2,0:T(8,128)(2,1)}, s32[2]{0:T(128)}, /*in...) while((s32[]{:T(128)}, f32[1024,3,64]{0,2,1:T(8,128)S(1)}, ...), condition=%wide.region_18.19_spmd.clone, body=%wide.region_16.18_spmd.clone.sunk | while | flops 1026392576 | bytes 66714016 | solution.py:83
  342.4 14.3 %while.66 = (s32[]{:T(128)}, bf16[2,512,3,64]{1,3,2,0:T(8,128)(2,1)}, s32[2]{0:T(128)S(1)}, bf16[1024,3,64]{0,2,1:T(8,128)(2,1)S(1)}, bf16[1024,3,64]{0,2,1:T(8,...) while((s32[]{:T(128)}, ...), condition=%wide.region_4.5_spmd.clone, body=%wide.region_1.4_spmd.clone.sunk | while | flops 415334912 | bytes 23261408 | solution.py:46
  361.5 38.9 %reduce-scatter.23.cloned.1.call-done = f32[256,768]{1,0:T(8,128)} async-done(((f32[1024,768]{1,0:T(8,128)}), f32[256,768]{1,0:T(8,128)}) %reduce-scatter.23.cloned.1.call-update) | async-done | bytes 786448 | tf_op jit(solution)/shard_map/reduce_scatter | solution.py:269
  400.5 63.0 %reduce-scatter.15.cloned.1.call-done = f32[256,768]{1,0:T(8,128)} async-done(((f32[1024,768]{1,0:T(8,128)}), f32[256,768]{1,0:T(8,128)}) %reduce-scatter.15.cloned.1.call-update) | async-done | bytes 786448 | tf_op jit(solution)/shard_map/reduce_scatter | solution.py:181
  463.5 65.0 %all-gather.11.cloned.1.call-done = f32[1024,768]{1,0:T(8,128)} async-done(((f32[256,768]{1,0:T(8,128)}), f32[1024,768]{1,0:T(8,128)}) %all-gather.11.cloned.1.call-update) | async-done | bytes 3145744 | tf_op jit(solution)/shard_map/all_gather | solution.py:270
  531.6 60.7 %all-gather.5.cloned.1.call-done = f32[1024,768]{1,0:T(8,128)} async-done(((f32[256,768]{1,0:T(8,128)}), f32[1024,768]{1,0:T(8,128)}) %all-gather.5.cloned.1.call-update) | async-done | bytes 3145744 | tf_op jit(solution)/shard_map/all_gather | solution.py:182
  592.3 5.6 multiply_reduce_fusion.4
  601.9 6.2 fusion.72
  612.8 5.6 fusion.73
  628.3 38.9 %reduce-scatter.17.cloned.1.call-done = f32[256,768]{1,0:T(8,128)} async-done(((f32[1024,768]{1,0:T(8,128)}), f32[256,768]{1,0:T(8,128)}) %reduce-scatter.17.cloned.1.call-update) | async-done | bytes 786448 | tf_op jit(solution)/shard_map/reduce_scatter | solution.py:189
  669.8 11.5 %collective-permute-done = bf16[256,768]{1,0:T(8,128)(2,1)S(1)} collective-permute-done((bf16[256,768]{1,0:T(8,128)(2,1)S(1)}, bf16[256,768]{1,0:T(8,128)(2,1)S(1)}, u32[]{:S(2)}, u32[]{:S(2)}) %collective-permute-start) | collective-permute-done | bytes 393248 | tf_op jit(solution)/shard_map/ppermute | solution.py:205
  687.9 17.4 %reduce-scatter.37.cloned.1.call-done = f32[96,192]{1,0:T(8,128)} async-done(((f32[768,192]{1,0:T(8,128)}), f32[96,192]{1,0:T(8,128)}) %reduce-scatter.37.cloned.1.call-update) | async-done | bytes 73744
  706.9 12.6 %all-reduce.2 = (f32[768]{0:T(1024)S(1)}, f32[768]{0:T(1024)S(1)}) all-reduce(f32[768]{0:T(1024)S(1)} %get-tuple-element.302, f32[768]{0:T(1024)S(1)} %copy-done.61), channel_id=7, replica_groups=mesh['dp'=8,'mp'=4] {'dp'}, use_global_device_ids=true, to_apply=%region_22.23.clone | all-reduce | flops 1536 | bytes 12288
  726.2 21.4 %reduce-scatter.35.cloned.1.call-done = f32[512,96]{0,1:T(8,128)} async-done(((f32[512,768]{0,1:T(8,128)}), f32[512,96]{0,1:T(8,128)}) %reduce-scatter.35.cloned.1.call-update) | async-done | bytes 196624 | tf_op jit(solution)/shard_map/reduce_scatter | solution.py:247
  747.7 42.2 %reduce-scatter.31.cloned.1.call-done = f32[96,512]{1,0:T(8,128)} async-done(((f32[768,512]{1,0:T(8,128)}), f32[96,512]{1,0:T(8,128)}) %reduce-scatter.31.cloned.1.call-update) | async-done | bytes 196624 | tf_op jit(solution)/shard_map/reduce_scatter | solution.py:244
  789.9 42.4 %reduce-scatter.33.cloned.1.call-done = f32[96,512]{1,0:T(8,128)} async-done(((f32[768,512]{1,0:T(8,128)}), f32[96,512]{1,0:T(8,128)}) %reduce-scatter.33.cloned.1.call-update) | async-done | bytes 196624 | tf_op jit(solution)/shard_map/reduce_scatter | solution.py:245
  832.3 38.6 %reduce-scatter.29.cloned.1.call-done = f32[96,192]{1,0:T(8,128)} async-done(((f32[768,192]{1,0:T(8,128)}), f32[96,192]{1,0:T(8,128)}) %reduce-scatter.29.cloned.1.call-update) | async-done | bytes 73744 | tf_op jit(solution)/shard_map/reduce_scatter | solution.py:278
  870.8 38.6 %reduce-scatter.25.cloned.1.call-done = f32[96,192]{1,0:T(8,128)} async-done(((f32[768,192]{1,0:T(8,128)}), f32[96,192]{1,0:T(8,128)}) %reduce-scatter.25.cloned.1.call-update) | async-done | bytes 73744 | tf_op jit(solution)/shard_map/reduce_scatter | solution.py:276
  909.4 38.6 %reduce-scatter.27.cloned.1.call-done = f32[96,192]{1,0:T(8,128)} async-done(((f32[768,192]{1,0:T(8,128)}), f32[96,192]{1,0:T(8,128)}) %reduce-scatter.27.cloned.1.call-update) | async-done | bytes 73744 | tf_op jit(solution)/shard_map/reduce_scatter | solution.py:277
  (310 shorter events, 126.9 us)
Async XLA Ops:
  7.2 159.6 %copy-start = (bf16[768,512]{1,0:T(8,128)(2,1)S(1)}, bf16[768,512]{1,0:T(8,128)(2,1)}, u32[]{:S(2)}) copy-start(bf16[768,512]{1,0:T(8,128)(2,1)} %param.26) | copy-start | bytes 2359300
  7.2 89.3 %reduce-scatter.19.cloned.1.call-start = ((), (), s32[]{:S(2)}) async-start(), calls=%async_computation.15 | async-start | bytes 3932160 | tf_op jit(solution)/shard_map/reduce_scatter | solution.py:185
  31.1 130.6 %copy-start.1 = (bf16[1024,768]{1,0:T(8,128)(2,1)S(1)}, bf16[1024,768]{1,0:T(8,128)(2,1)}, u32[]{:S(2)}) copy-start(bf16[1024,768]{1,0:T(8,128)(2,1)} %param.18) | copy-start | bytes 4718596
  33.4 128.2 %all-gather.7.cloned.1.call-start = ((), (), s32[]{:S(2)}) async-start(), calls=%async_computation.16 | async-start | bytes 3932160 | tf_op jit(solution)/shard_map/all_gather | solution.py:186
  96.6 138.7 %reduce-scatter.21.cloned.1.call-start = ((), (), s32[]{:S(2)}) async-start(), calls=%async_computation.17 | async-start | bytes 3932160 | tf_op jit(solution)/shard_map/reduce_scatter | solution.py:237
  176.2 124.0 %all-gather.9.cloned.1.call-start = ((), (), s32[]{:S(2)}) async-start(), calls=%async_computation.18 | async-start | bytes 3932160 | tf_op jit(solution)/shard_map/all_gather | solution.py:238
  235.3 165.2 %reduce-scatter.23.cloned.1.call-start = ((), (), s32[]{:S(2)}) async-start(), calls=%async_computation.19 | async-start | bytes 3932160 | tf_op jit(solution)/shard_map/reduce_scatter | solution.py:269
  341.4 122.1 %reduce-scatter.15.cloned.1.call-start = ((), (), s32[]{:S(2)}) async-start(), calls=%async_computation.12 | async-start | bytes 3932160 | tf_op jit(solution)/shard_map/reduce_scatter | solution.py:181
  361.4 167.1 %copy-start.52 = (f32[768]{0:T(1024)S(1)}, f32[768]{0:T(1024)}, u32[]{:S(2)}) copy-start(f32[768]{0:T(1024)} %copy-done.51) | copy-start | bytes 9220
  361.5 167.1 %copy-start.54 = (f32[1024]{0:T(1024)S(1)}, f32[1024]{0:T(1024)}, u32[]{:S(2)}) copy-start(f32[1024]{0:T(1024)} %copy-done.53) | copy-start | bytes 12292
  361.5 167.1 %all-gather.11.cloned.1.call-start = ((), (), s32[]{:S(2)}) async-start(), calls=%async_computation.20 | async-start | bytes 3932160 | tf_op jit(solution)/shard_map/all_gather | solution.py:270
  400.4 131.2 %copy-start.58 = (f32[1024]{0:T(1024)S(1)}, f32[1024]{0:T(1024)}, u32[]{:S(2)}) copy-start(f32[1024]{0:T(1024)} %copy-done.57) | copy-start | bytes 12292
  400.5 191.9 %all-gather.5.cloned.1.call-start = ((), (), s32[]{:S(2)}) async-start(), calls=%async_computation.13 | async-start | bytes 3932160 | tf_op jit(solution)/shard_map/all_gather | solution.py:182
  463.5 203.8 %reduce-scatter.17.cloned.1.call-start = ((), (), s32[]{:S(2)}) async-start(), calls=%async_computation.14 | async-start | bytes 3932160 | tf_op jit(solution)/shard_map/reduce_scatter | solution.py:189
  608.2 97.1 %reduce-scatter.37.cloned.1.call-start = ((), (), s32[]{:S(2)}) async-start(), calls=%async_computation.27 | async-start | bytes 884736
  612.8 134.9 %reduce-scatter.35.cloned.1.call-start = ((), (), s32[]{:S(2)}) async-start(), calls=%async_computation.26 | async-start | bytes 1769472 | tf_op jit(solution)/shard_map/reduce_scatter | solution.py:247
  618.5 171.4 %reduce-scatter.31.cloned.1.call-start = ((), (), s32[]{:S(2)}) async-start(), calls=%async_computation.24 | async-start | bytes 1769472 | tf_op jit(solution)/shard_map/reduce_scatter | solution.py:244
  621.0 211.3 %reduce-scatter.33.cloned.1.call-start = ((), (), s32[]{:S(2)}) async-start(), calls=%async_computation.25 | async-start | bytes 1769472 | tf_op jit(solution)/shard_map/reduce_scatter | solution.py:245
  625.1 245.8 %reduce-scatter.29.cloned.1.call-start = ((), (), s32[]{:S(2)}) async-start(), calls=%async_computation.23 | async-start | bytes 884736 | tf_op jit(solution)/shard_map/reduce_scatter | solution.py:278
  626.7 282.7 %reduce-scatter.25.cloned.1.call-start = ((), (), s32[]{:S(2)}) async-start(), calls=%async_computation.21 | async-start | bytes 884736 | tf_op jit(solution)/shard_map/reduce_scatter | solution.py:276
  628.3 319.7 %reduce-scatter.27.cloned.1.call-start = ((), (), s32[]{:S(2)}) async-start(), calls=%async_computation.22 | async-start | bytes 884736 | tf_op jit(solution)/shard_map/reduce_scatter | solution.py:277
  668.7 12.6 %collective-permute-start = (bf16[256,768]{1,0:T(8,128)(2,1)S(1)}, bf16[256,768]{1,0:T(8,128)(2,1)S(1)}, u32[]{:S(2)}, u32[]{:S(2)}) collective-permute-start(bf16[256,768]{1,0:T(8,128)(2,1)S(1)} %select_convert_fusion), channel_id=1, source_target_pairs={{0,1},{1,2},{2,3},{3,0},{4,5},{5,6},{6,7},{7,4},{8,9},{9,10},{10,1... | collective-permute-start | bytes 1179656 | tf_op jit(solution)/shard_map/ppermute | solution.py:205
  681.3 39.4 %collective-permute-start.1 = (bf16[256,768]{1,0:T(8,128)(2,1)S(1)}, bf16[256,768]{1,0:T(8,128)(2,1)}, u32[]{:S(2)}, u32[]{:S(2)}) collective-permute-start(bf16[256,768]{1,0:T(8,128)(2,1)S(1)} %collective-permute-done), channel_id=1, source_target_pairs={{0,1},{1,2},{2,3},{3,0},{4,5},{5,6},{6,7},{7,4},{8,9},{9,10},{10,1... | collective-permute-start | bytes 1179656 | tf_op jit(solution)/shard_map/ppermute | solution.py:205
  682.5 39.3 %collective-permute-start.2 = (bf16[256,768]{1,0:T(8,128)(2,1)S(1)}, bf16[256,768]{1,0:T(8,128)(2,1)}, u32[]{:S(2)}, u32[]{:S(2)}) collective-permute-start(bf16[256,768]{1,0:T(8,128)(2,1)S(1)} %select_convert_fusion), channel_id=1, source_target_pairs={{0,3},{1,0},{2,1},{3,2},{4,7},{5,4},{6,5},{7,6},{8,11},{9,8},{10,9... | collective-permute-start | bytes 1179656 | tf_op jit(solution)/shard_map/ppermute | solution.py:207
  (77 other events, 706.4 us)
Sparse Core Ops, SparseCore 0:
  33.5 62.9 reduce-scatter.18
  98.1 63.5 all-gather.6
  176.3 58.8 reduce-scatter.20
  236.7 63.5 all-gather.8
  341.5 58.8 reduce-scatter.22
  403.2 60.2 reduce-scatter.14
  465.0 63.5 all-gather.10
  530.2 62.1 all-gather.4
  608.3 58.8 reduce-scatter.16
  670.2 35.0 reduce-scatter.36
  709.2 38.4 reduce-scatter.34
  751.4 38.4 reduce-scatter.30
  793.8 38.4 reduce-scatter.32
  835.8 34.9 reduce-scatter.28
  874.4 34.9 reduce-scatter.24
  913.0 34.9 reduce-scatter.26
